TPU v7x, 32 devices: a whole 2x2x4 slice. The times are simulated.
32 devices in a mesh: dp: 16 (over z, y, core), owner: 2 (over x).
Axes of the slice: x: 2, y: 2, z: 4, core: 2. Of those that a mesh axis runs over, the one named last changes fastest.
Arguments:
- hidden: bfloat16 [2048, 4096], P('dp'), may hold values from -6 to 6
- norm_gain: float32 [4096], replicated, may hold values from 0.3 to 3
- cotangent: bfloat16 [2048, 6144], P('dp'), may hold values from -30 to 30
Outputs:
- update: bfloat16 [6144, 4096], P('dp', 'owner')
All inputs are finite; a program needn't handle non-finite values. Where the computation divides by a largest or mean magnitude, that divisor is 1e-20 or more.
Results may differ from a plain program's by a relative error of at most 0.014.
Values may be sent and summed in bfloat16 or wider, within the bound.
A program may use at most 128 MiB of HBM per device.

v0:
```python
import jax
import jax.numpy as jnp
from jax import lax
from jax.sharding import PartitionSpec as P

TILE = 1024


DAMPING = 0.1


def contract(left, right, left_dim, right_dim):
    return lax.dot_general(
        left, right, (((left_dim,), (right_dim,)), ((), ())), preferred_element_type=jnp.float32
    )


def inverse_of(piece, tokens):
    identity = jnp.eye(TILE, dtype=jnp.float32)
    matrix = contract(piece, piece, 0, 0) / tokens + DAMPING * identity
    scale = 1.0 / jnp.max(jnp.sum(jnp.abs(matrix), axis=1))
    first = 2.0 * scale * identity - (scale * scale) * matrix
    first_low = first.astype(jnp.bfloat16)
    matrix_low = matrix.astype(jnp.bfloat16)
    product = contract(first_low, matrix_low, 1, 0).astype(jnp.bfloat16)
    return (2.0 * first - contract(product, first_low, 1, 0)).astype(jnp.bfloat16)


def shards(hidden, norm_gain, cotangent):
    owners = lax.axis_size("owner")
    position = lax.axis_index("owner")
    groups = lax.axis_size("dp")
    group = lax.axis_index("dp")
    tokens_here = hidden.shape[0]
    tokens = tokens_here * groups
    width = hidden.shape[1]
    out_width = cotangent.shape[1]
    strip = out_width // groups
    own = width // owners
    in_width = max(own, TILE)

    firsts = jnp.array([(g * strip) // TILE for g in range(groups)], jnp.int32)
    lasts = jnp.array([((g + 1) * strip - 1) // TILE for g in range(groups)], jnp.int32)
    odd = lax.rem(position, 2) == 1
    wanted = jnp.where(odd, lasts, firsts)
    outgoing = jnp.stack(
        [
            lax.dynamic_slice_in_dim(cotangent, wanted[g] * TILE, TILE, 1)
            for g in range(groups)
        ]
    )
    out_piece = lax.all_to_all(outgoing, "dp", 0, 0, tiled=True).reshape(tokens, TILE)

    states = hidden.astype(jnp.float32)
    normed = (
        states * lax.rsqrt(jnp.mean(states * states, axis=1, keepdims=True) + 1e-05) * norm_gain
    ).astype(jnp.bfloat16)
    in_start = (position * own) // TILE * TILE
    mine = lax.dynamic_slice_in_dim(normed, in_start, in_width, 1)
    in_piece = lax.all_gather(mine, "dp", axis=0, tiled=True)

    out_inverse = inverse_of(out_piece, tokens)
    padded = jnp.pad(out_inverse, ((0, 0), (strip, strip)))
    offset = group * strip - wanted[group] * TILE
    strip_inverse = lax.dynamic_slice_in_dim(padded, offset + strip, strip, 1)
    part = contract(out_piece, strip_inverse, 1, 0).astype(jnp.bfloat16)
    other = lax.ppermute(part, "owner", [(o, o ^ 1) for o in range(owners)])
    column_block = (group * strip + jnp.arange(strip, dtype=jnp.int32)) // TILE
    pre_out = jnp.where((column_block == wanted[group])[None, :], part, other)

    results = []
    for block in range(in_width // TILE):
        piece = in_piece[:, block * TILE : (block + 1) * TILE]
        inverse = inverse_of(piece, tokens)
        if own < TILE:
            inverse = lax.dynamic_slice_in_dim(inverse, position * own - in_start, own, 1)
        cross = contract(pre_out, piece, 0, 0).astype(jnp.bfloat16)
        results.append(contract(cross, inverse, 1, 0))
    summed = jnp.concatenate(results, axis=1)
    squares = lax.psum(jnp.sum(summed * summed), ("dp", "owner"))
    return (summed * lax.rsqrt(squares / (width * out_width) + 1e-06)).astype(jnp.bfloat16)


def solution(mesh):
    in_specs = (P("dp", None), P(), P("dp", None))
    out_specs = P("dp", "owner")
    return jax.shard_map(shards, mesh=mesh, in_specs=in_specs, out_specs=out_specs, check_vma=False)
```

profile of v0, /device:TPU:0, one launch (start us, length us, event | category | flops | bytes accessed | tf_op | source)
XLA Modules:
  0.0 321.7 jit_solution(2514432359440347336)
XLA Ops:
  6.6 2.9 convert_element_type.64
  9.5 1.5 multiply_reduce_fusion.1
  11.1 2.2 fusion.96
  24.1 1.6 constant_dynamic-slice_fusion
  25.7 1.8 copy.23
  27.6 1.8 copy.24
  29.4 1.8 copy.25
  31.2 1.8 copy.26
  33.0 1.8 copy.27
  34.8 1.8 copy.28
  36.6 1.8 copy.29
  38.4 1.8 copy.30
  43.0 1.7 bitcast_dynamic-update-slice_fusion.15
  44.7 1.7 bitcast_dynamic-update-slice_fusion.14
  46.3 1.7 bitcast_dynamic-update-slice_fusion.13
  48.0 1.7 bitcast_dynamic-update-slice_fusion.12
  49.7 1.7 bitcast_dynamic-update-slice_fusion.11
  51.4 1.7 bitcast_dynamic-update-slice_fusion.10
  60.3 7.5 %all-to-all-start = ((bf16[16,128,1024]{1,2,0:T(8,128)(2,1)}), bf16[16,128,1024]{1,2,0:T(8,128)(2,1)}, u32[]{:S(2)}, u32[]{:S(2)}) async-start(bf16[16,128,1024]{1,2,0:T(8,128)(2,1)} %bitcast_dynamic-update-slice_fusion), calls=%async_computation | async-start | bytes 8388608 | tf_op jit(solution)/shard_map/all_to_all | solution.py:52
  69.0 91.5 %all-to-all-done = bf16[16,128,1024]{1,2,0:T(8,128)(2,1)} async-done(((bf16[16,128,1024]{1,2,0:T(8,128)(2,1)}), bf16[16,128,1024]{1,2,0:T(8,128)(2,1)}, u32[]{:S(2)}, u32[]{:S(2)}) %all-to-all-start) | async-done | bytes 4194336 | tf_op jit(solution)/shard_map/all_to_all | solution.py:52
  160.5 9.9 %abs_reduce_fusion.2 = (f32[1024]{0:T(1024)S(1)}, f32[1024,1024]{0,1:T(8,128)}) fusion(bf16[16,128,1024]{1,2,0:T(8,128)(2,1)} %all-to-all-done), kind=kOutput, calls=%fused_computation.12 | convolution fusion | flops 4301257728 | bytes 8392704 | tf_op jit(solution)/shard_map/dot_general | solution.py:13
  171.7 6.6 %copy.39 = bf16[16,128,1024]{2,1,0:T(8,128)(2,1)} copy(bf16[16,128,1024]{1,2,0:T(8,128)(2,1)} %all-to-all-done) | data formatting | bytes 8388608 | tf_op jit(solution)/shard_map/all_to_all | solution.py:52
  178.2 11.9 %subtract_convert_fusion.2 = bf16[1024,1024]{0,1:T(8,128)(2,1)} fusion(f32[1024,1024]{0,1:T(8,128)} %get-tuple-element.41, f32[]{:T(128)S(6)} %mul.246, f32[]{:T(128)S(6)} %mul.243), kind=kOutput, calls=%fused_computation.10 | convolution fusion | flops 4314890240 | bytes 6291464 | tf_op jit(solution)/shard_map/dot_general | solution.py:13
  190.1 4.8 %convolution_convert_fusion = bf16[2048,384]{1,0:T(8,128)(2,1)S(1)} fusion(bf16[2048,1024]{1,0:T(8,128)(2,1)} %bitcast.59, s32[]{:T(128)S(6)} %select_n.104, bf16[1024,1024]{0,1:T(8,128)(2,1)} %subtract_convert_fusion.2), kind=kOutput, calls=%fused_computation.29 | convolution fusion | flops 1611399168 | bytes 7864324 | tf_op jit(solution)/shard_map/dot_general | solution.py:13
  194.9 1.5 collective-permute-start
  196.4 10.1 %abs_reduce_fusion.1 = (f32[1024]{0:T(1024)S(1)}, f32[1024,1024]{0,1:T(8,128)}) fusion(bf16[2048,2048]{1,0:T(8,128)(2,1)} %all-gather.2.cloned.1.call-done), kind=kOutput, calls=%fused_computation.9 | convolution fusion | flops 4301257728 | bytes 8392704 | tf_op jit(solution)/shard_map/dot_general | solution.py:13
  207.8 10.3 %abs_reduce_fusion = (f32[1024]{0:T(1024)S(1)}, f32[1024,1024]{0,1:T(8,128)}) fusion(bf16[2048,2048]{1,0:T(8,128)(2,1)} %all-gather.2.cloned.1.call-done), kind=kOutput, calls=%fused_computation.6 | convolution fusion | flops 4301257728 | bytes 8392704 | tf_op jit(solution)/shard_map/dot_general | solution.py:13
  219.4 12.3 %subtract_convert_fusion.1 = bf16[1024,1024]{0,1:T(8,128)(2,1)} fusion(f32[]{:T(128)S(6)} %mul.261, f32[1024,1024]{0,1:T(8,128)} %get-tuple-element.43, f32[]{:T(128)S(6)} %mul.258), kind=kOutput, calls=%fused_computation.7 | convolution fusion | flops 4328521728 | bytes 6291464 | tf_op jit(solution)/shard_map/dot_general | solution.py:13
  231.7 12.4 %subtract_convert_fusion = bf16[1024,1024]{0,1:T(8,128)(2,1)} fusion(f32[]{:T(128)S(6)} %mul.268, f32[1024,1024]{0,1:T(8,128)} %get-tuple-element.39, f32[]{:T(128)S(6)} %mul.265), kind=kOutput, calls=%fused_computation.4 | convolution fusion | flops 4328521728 | bytes 6291464 | tf_op jit(solution)/shard_map/dot_general | solution.py:13
  244.1 6.0 %fusion.101 = f32[384,1024]{1,0:T(8,128)S(1)} fusion(bf16[1024,1024]{0,1:T(8,128)(2,1)} %subtract_convert_fusion.1, bf16[2048,2048]{1,0:T(8,128)(2,1)} %all-gather.2.cloned.1.call-done, bf16[2048,384]{1,0:T(8,128)(2,1)S(1)} %convolution_convert_fusion, bf16[2048,384]{1,0:T(8,128)(2,1)} %collective-permute-done, pred[384]{0:T(512)(128)(4,1)S(1)} %fusion.105), kind=kOutput, calls=%fused_computation.60 | convolution fusion | flops 2417098752 | bytes 11010432 | tf_op jit(solution)/shard_map/dot_general | solution.py:13
  250.1 6.4 %fusion.98 = f32[384,1024]{1,0:T(8,128)S(1)} fusion(bf16[1024,1024]{0,1:T(8,128)(2,1)} %subtract_convert_fusion, bf16[2048,2048]{1,0:T(8,128)(2,1)} %all-gather.2.cloned.1.call-done, bf16[2048,384]{1,0:T(8,128)(2,1)} %copy-done.9, bf16[2048,384]{1,0:T(8,128)(2,1)} %collective-permute-done, pred[384]{0:T(512)(128)(4,1)S(1)} %fusion.105), kind=kOutput, calls=%fused_computation.59 | convolution fusion | flops 2417098752 | bytes 11010432 | tf_op jit(solution)/shard_map/dot_general | solution.py:13
  257.8 54.5 %psum.7 = f32[]{:T(128)} all-reduce(f32[]{:T(128)} %multiply_reduce_fusion), channel_id=1, replica_groups=mesh['dp'=16,'owner'=2] {'dp','owner'}, use_global_device_ids=true, to_apply=%region_8.9 | all-reduce | flops 1 | bytes 8 | tf_op jit(solution)/shard_map/psum | solution.py:80
  (52 shorter events, 16.0 us)
Async XLA Ops:
  6.5 6.8 %copy-start.7 = (s32[16]{0:T(128)S(1)}, s32[16]{0:T(128)}, u32[]{:S(2)}) copy-start(s32[16]{0:T(128)} %constant.105.clone) | copy-start | bytes 196
  6.5 6.8 %copy-start.8 = (s32[16]{0:T(128)S(1)}, s32[16]{0:T(128)}, u32[]{:S(2)}) copy-start(s32[16]{0:T(128)} %constant.106.clone) | copy-start | bytes 196
  6.5 4.5 %copy-start.6 = (f32[4096]{0:T(1024)S(1)}, f32[4096]{0:T(1024)}, u32[]{:S(2)}) copy-start(f32[4096]{0:T(1024)} %param.6) | copy-start | bytes 49156
  6.5 17.6 %copy-start = (bf16[128,6144]{1,0:T(8,128)(2,1)S(1)}, bf16[128,6144]{1,0:T(8,128)(2,1)}, u32[]{:S(2)}) copy-start(bf16[128,6144]{1,0:T(8,128)(2,1)} %param.7) | copy-start | bytes 4718596
  6.5 189.9 %all-gather.2.cloned.1.call-start = ((), (), s32[]{:S(2)}) async-start(), calls=%async_computation.1 | async-start | bytes 8912896 | tf_op jit(solution)/shard_map/all_gather | solution.py:60
  25.7 14.5 %copy-start.1 = (bf16[128,1024]{1,0:T(8,128)(2,1)S(1)}, bf16[128,1024]{1,0:T(8,128)(2,1)}, u32[]{:S(2)}) copy-start(bf16[128,1024]{1,0:T(8,128)(2,1)} %get-tuple-element.11) | copy-start | bytes 786436
  41.9 13.4 %copy-start.2 = (bf16[128,1024]{0,1:T(8,128)(2,1)S(1)}, bf16[128,1024]{0,1:T(8,128)(2,1)}, u32[]{:S(2)}) copy-start(bf16[128,1024]{0,1:T(8,128)(2,1)} %copy.32) | copy-start | bytes 786436
  42.1 12.5 %copy-start.3 = (bf16[128,1024]{0,1:T(8,128)(2,1)S(1)}, bf16[128,1024]{0,1:T(8,128)(2,1)}, u32[]{:S(2)}) copy-start(bf16[128,1024]{0,1:T(8,128)(2,1)} %copy.31) | copy-start | bytes 786436
  42.3 11.5 %copy-start.4 = (bf16[128,1024]{0,1:T(8,128)(2,1)S(1)}, bf16[128,1024]{0,1:T(8,128)(2,1)}, u32[]{:S(2)}) copy-start(bf16[128,1024]{0,1:T(8,128)(2,1)} %copy.30) | copy-start | bytes 786436
  42.4 10.7 %copy-start.5 = (bf16[128,1024]{0,1:T(8,128)(2,1)S(1)}, bf16[128,1024]{0,1:T(8,128)(2,1)}, u32[]{:S(2)}) copy-start(bf16[128,1024]{0,1:T(8,128)(2,1)} %copy.29) | copy-start | bytes 786436
  60.3 100.1 %all-to-all-start = ((bf16[16,128,1024]{1,2,0:T(8,128)(2,1)}), bf16[16,128,1024]{1,2,0:T(8,128)(2,1)}, u32[]{:S(2)}, u32[]{:S(2)}) async-start(bf16[16,128,1024]{1,2,0:T(8,128)(2,1)} %bitcast_dynamic-update-slice_fusion), calls=%async_computation | async-start | bytes 8388608 | tf_op jit(solution)/shard_map/all_to_all | solution.py:52
  194.9 49.2 %copy-start.9 = (bf16[2048,384]{1,0:T(8,128)(2,1)}, bf16[2048,384]{1,0:T(8,128)(2,1)S(1)}, u32[]{:S(2)}) copy-start(bf16[2048,384]{1,0:T(8,128)(2,1)S(1)} %convolution_convert_fusion) | copy-start | bytes 4718596
  194.9 49.2 %collective-permute-start = (bf16[2048,384]{1,0:T(8,128)(2,1)S(1)}, bf16[2048,384]{1,0:T(8,128)(2,1)}, u32[]{:S(2)}, u32[]{:S(2)}) collective-permute-start(bf16[2048,384]{1,0:T(8,128)(2,1)S(1)} %convolution_convert_fusion), channel_id=1, source_target_pairs={{0,1},{1,0},{2,3},{3,2},{4,5},{5,4},{6,7},{7,6},{8,9},{9,8},{10,11... | collective-permute-start | bytes 4718600 | tf_op jit(solution)/shard_map/ppermute | solution.py:67
Sparse Core Ops, SparseCore 0:
  13.4 105.0 all-gather.1
where the time goes:
time: 328 us; the launch traced here: 322 us
  waiting for transfers between devices  91.5 us (28%)
  matrix products  84.1 us (26%)
  blocking collectives  54.5 us (17%)
  local copies, waits for them, and re-layouts  43.5 us (13%)
  between operations  27.3 us (8%)
  other arithmetic  11.9 us (4%)
  starting transfers between devices  9.01 us (3%)
    all_to_all x1, waiting for transfers between devices, shards(): lax.all_to_all(outgoing, 'dp', 0, 0, tiled=True).reshape(tokens, TILE)  91.5 us
    dot_general x9, matrix products, contract(): lax.dot_general(left, right, (((left_dim,), (right_dim,)), ((), ())), pre...  84.1 us
    psum x1, blocking collectives, shards(): squares = lax.psum(jnp.sum(summed * summed), ('dp', 'owner'))  54.5 us
    dynamic_slice x17, local copies, waits for them, and re-layouts, shards(): lax.dynamic_slice_in_dim(cotangent, wanted[g] * TILE, TILE, 1)  18.8 us
    unnamed x35, local copies, waits for them, and re-layouts  16.7 us
    all_to_all x1, starting transfers between devices, shards(): lax.all_to_all(outgoing, 'dp', 0, 0, tiled=True).reshape(tokens, TILE)  7.47 us
    all_to_all x1, local copies, waits for them, and re-layouts, shards(): lax.all_to_all(outgoing, 'dp', 0, 0, tiled=True).reshape(tokens, TILE)  6.56 us
  transfers between devices with their start and end apart: 3, of which 1 were waited for; matrix products, arithmetic and copies ran while one was open for 37% of the time, Pallas kernels for 0%

commit v1 on v0

--- a/solution.py
+++ b/solution.py
@@ -1,6 +1,10 @@
+import functools
+
 import jax
 import jax.numpy as jnp
 from jax import lax
+from jax.experimental import pallas as pl
+from jax.experimental.pallas import tpu as pltpu
 from jax.sharding import PartitionSpec as P
 
 TILE = 1024
@@ -81,7 +85,590 @@
     return (summed * lax.rsqrt(squares / (width * out_width) + 1e-06)).astype(jnp.bfloat16)
 
 
+MESH = pl.DeviceIdType.MESH
+UNIT = TILE // 4
+CHUNK = 128
+
+
+def flipped(value, mask):
+    for bit in range(mask.bit_length()):
+        if (mask >> bit) & 1:
+            value = value + (1 - 2 * ((value // 2**bit) % 2)) * 2**bit
+    return value
+
+
+def matrix_chunk(gram, tokens, i):
+    shape = (CHUNK, TILE)
+    row = lax.broadcasted_iota(jnp.int32, shape, 0) + i * CHUNK
+    column = lax.broadcasted_iota(jnp.int32, shape, 1)
+    rows = pl.ds(pl.multiple_of(i * CHUNK, CHUNK), CHUNK)
+    return gram[rows, :] * (1.0 / tokens) + jnp.where(row == column, DAMPING, 0.0)
+
+
+def scaled_factor(gram, low, tokens):
+    def add(i, total):
+        return total + jnp.sum(jnp.abs(matrix_chunk(gram, tokens, i)), axis=0, keepdims=True)
+
+    sums = lax.fori_loop(0, TILE // CHUNK, add, jnp.zeros((1, TILE), jnp.float32))
+    scale = 1.0 / jnp.max(sums, axis=1, keepdims=True)
+
+    def put(i, carry):
+        rows = pl.ds(pl.multiple_of(i * CHUNK, CHUNK), CHUNK)
+        low[rows, :] = (scale * matrix_chunk(gram, tokens, i)).astype(jnp.bfloat16)
+        return carry
+
+    lax.fori_loop(0, TILE // CHUNK, put, 0)
+    return scale
+
+
+def whole_kernel(
+    sizes,
+    hidden_ref,
+    gain_ref,
+    cotangent_ref,
+    update_ref,
+    states,
+    cbuf,
+    nbuf,
+    other_n,
+    gram_c,
+    gram_n,
+    low_c,
+    low_n,
+    pre,
+    give,
+    cross,
+    mine,
+    theirs,
+    arrived,
+    squares,
+    load_sem,
+    c_send,
+    c_x,
+    c_core,
+    c_recv,
+    n_core,
+    n_up,
+    n_down,
+    n_y,
+    n_recv,
+    pre_send,
+    pre_recv,
+    swap_send,
+    swap_recv,
+    sq_send,
+    sq_recv,
+):
+    groups, owners, tokens_here, width, out_width = sizes
+    tokens = groups * tokens_here
+    line = groups // 4
+    strip = out_width // groups
+    own = width // owners
+    me = lax.axis_index("dp")
+    x = lax.axis_index("owner")
+    z = me // 4
+    y = (me // 2) % 2
+    c = me % 2
+    devices = groups * owners
+    flat = me * owners + x
+
+    def slot_of(y_, z_, c_):
+        return (y_ * line + z_) * 2 + c_
+
+    def device(x_, y_, z_, c_):
+        return ((z_ * 2 + y_) * 2 + c_, x_)
+
+    def block_of(p):
+        return 3 * (p // 4) + (p % 4 + 1) // 2
+
+    def remote(src, dst, send, recv, target):
+        return pltpu.make_async_remote_copy(
+            src_ref=src,
+            dst_ref=dst,
+            send_sem=send,
+            recv_sem=recv,
+            device_id=target,
+            device_id_type=MESH,
+        )
+
+    own_slot = slot_of(y, z, c)
+    core_slot = slot_of(y, z, 1 - c)
+    core_peer = device(x, y, z, 1 - c)
+    x_peer = device(1 - x, y, z, c)
+
+    load = pltpu.make_async_copy(hidden_ref, states, load_sem.at[0])
+    load.start()
+
+    barrier = pltpu.get_barrier_semaphore()
+
+    def greet(d, carry):
+        target = (flat + d) % devices
+        pl.semaphore_signal(
+            barrier, inc=1, device_id=(target // owners, target % owners), device_id_type=MESH
+        )
+        return carry
+
+    lax.fori_loop(1, devices, greet, 0)
+    pl.semaphore_wait(barrier, devices - 1)
+
+    def block_columns(y_, z_):
+        return pl.ds(pl.multiple_of(block_of(z_ * 2 + y_) * TILE, TILE), TILE)
+
+    def c_out(k):
+        zd = flipped(z, k)
+        yd = (y + x + z + zd) % 2
+        return remote(
+            cotangent_ref.at[:, block_columns(yd, zd)],
+            cbuf.at[own_slot],
+            c_send.at[k],
+            c_recv.at[own_slot],
+            device(x, yd, zd, c),
+        )
+
+    def c_in_slot(k, through):
+        zs = flipped(z, k)
+        ys = (y + x + through + z + zs) % 2
+        return slot_of(ys, zs, c)
+
+    def c_relay(slot, sems, target):
+        return remote(cbuf.at[slot], cbuf.at[slot], sems.at[slot], c_recv.at[slot], target)
+
+    for k in range(1, line):
+        c_out(k).start()
+
+    @pl.when(x == 1)
+    def _():
+        c_out(0).start()
+
+    local = pltpu.make_async_copy(
+        cotangent_ref.at[:, block_columns(y, z)], cbuf.at[own_slot], load_sem.at[1]
+    )
+    local.start()
+    c_own = remote(
+        cotangent_ref.at[:, block_columns(y, z)],
+        cbuf.at[own_slot],
+        c_core.at[own_slot],
+        c_recv.at[own_slot],
+        core_peer,
+    )
+    c_own.start()
+
+    load.wait()
+    part = 16
+    kept = pl.ds(pl.multiple_of(x * own + c * TILE, TILE), TILE)
+    passed = pl.ds(pl.multiple_of(x * own + (1 - c) * TILE, TILE), TILE)
+
+    def normalize(i, carry):
+        rows = pl.ds(pl.multiple_of(i * part, part), part)
+        full = states[rows, :].astype(jnp.float32)
+        factor = lax.rsqrt(jnp.sum(full * full, axis=1, keepdims=True) * (1.0 / width) + 1e-05)
+        for columns, put in ((passed, other_n), (kept, nbuf.at[own_slot])):
+            piece = states[rows, columns].astype(jnp.float32) * factor * gain_ref[:, columns]
+            put[rows, :] = piece.astype(jnp.bfloat16)
+        return carry
+
+    lax.fori_loop(0, tokens_here // part, normalize, 0)
+    n_pass = remote(other_n, nbuf.at[own_slot], n_core.at[0], n_recv.at[own_slot], core_peer)
+    n_pass.start()
+
+    def n_copy(slot, sems, target):
+        return remote(nbuf.at[slot], nbuf.at[slot], sems.at[slot], n_recv.at[slot], target)
+
+    def n_to_y(slot):
+        return n_copy(slot, n_y, device(x, 1 - y, z, c))
+
+    def n_to_up(slot):
+        return n_copy(slot, n_up, device(x, y, z + 1, c))
+
+    def n_to_down(slot):
+        return n_copy(slot, n_down, device(x, y, z - 1, c))
+
+    def own_out(slot, act):
+        act(n_to_y(slot))
+
+        @pl.when(z + 1 < line)
+        def _():
+            act(n_to_up(slot))
+
+        @pl.when(z > 0)
+        def _():
+            act(n_to_down(slot))
+
+    def start(copy):
+        copy.start()
+
+    def drain(copy):
+        copy.wait_send()
+
+    own_out(own_slot, start)
+    n_to_y(core_slot).wait_recv()
+    own_out(core_slot, start)
+
+    def line_source(i):
+        low = jnp.minimum(z, line - 1 - z)
+        near = i < 2 * low
+        distance = jnp.where(near, i // 2 + 1, i + 1 - low)
+        below = jnp.where(near, i % 2 == 0, z > low)
+        return jnp.where(below, z - distance, z + distance), below
+
+    def line_out(slot, below, act):
+        act(n_to_y(slot))
+
+        @pl.when(jnp.logical_and(below, z + 1 < line))
+        def _():
+            act(n_to_up(slot))
+
+        @pl.when(jnp.logical_and(jnp.logical_not(below), z > 0))
+        def _():
+            act(n_to_down(slot))
+
+    def line_step(i, carry):
+        zs, below = line_source(i)
+        for cs in range(2):
+            slot = slot_of(y, zs, cs)
+            n_to_y(slot).wait_recv()
+            line_out(slot, below, start)
+        return carry
+
+    def c_direct(k):
+        slot = c_in_slot(k, 0)
+        c_relay(slot, c_x, x_peer).wait_recv()
+        c_relay(slot, c_x, x_peer).start()
+        c_relay(slot, c_core, core_peer).start()
+
+    for k in range(1, line):
+        c_direct(k)
+
+    @pl.when(x == 1)
+    def _():
+        c_direct(0)
+
+    line_step(0, 0)
+
+    def c_shared(k):
+        slot = c_in_slot(k, 1)
+        c_relay(slot, c_core, core_peer).wait_recv()
+        c_relay(slot, c_core, core_peer).start()
+
+    for k in range(1, line):
+        c_shared(k)
+
+    @pl.when(x == 0)
+    def _():
+        c_shared(0)
+
+    def c_from_core(i, carry):
+        slot = 2 * i + 1 - c
+        c_relay(slot, c_core, core_peer).wait_recv()
+        return carry
+
+    lax.fori_loop(0, groups // 2, c_from_core, 0)
+    local.wait()
+
+    line_step(1, 0)
+    block_tokens = cbuf[...].reshape(tokens, TILE)
+    gram_c[...] = contract(block_tokens, block_tokens, 0, 0)
+    scale_c = scaled_factor(gram_c, low_c, tokens)
+    lax.fori_loop(2, line - 1, line_step, 0)
+
+    p = z * 2 + y
+    r = p % 4
+    edge = jnp.where(jnp.logical_or(r == 0, r == 3), 1, 0)
+    block = block_of(p)
+
+    def unit_of(k):
+        return edge * (3 * c + k * (1 - 2 * c)) + (1 - edge) * (2 * (r - 1) + c)
+
+    def place_of(k):
+        return 4 * block + unit_of(k) - 3 * p
+
+    def strip_columns(place):
+        return pl.ds(pl.multiple_of(place * UNIT, UNIT), UNIT)
+
+    def pre_copy(place, send, target):
+        view = pre.at[:, strip_columns(place)]
+        return remote(view, view, send, pre_recv.at[place], target)
+
+    def give_copy(k):
+        place = place_of(k) - 3 * (1 - 2 * y)
+        return remote(
+            give,
+            pre.at[:, strip_columns(place)],
+            pre_send.at[2],
+            pre_recv.at[place],
+            device(x, 1 - y, z, c),
+        )
+
+    def unit_value(k):
+        unit = unit_of(k)
+        first = low_c[:, pl.ds(pl.multiple_of(unit * UNIT, UNIT), UNIT)]
+        second = contract(low_c[...], first, 1, 0)
+        third = contract(low_c[...], second.astype(jnp.bfloat16), 1, 0)
+        row = lax.broadcasted_iota(jnp.int32, (TILE, UNIT), 0)
+        column = lax.broadcasted_iota(jnp.int32, (TILE, UNIT), 1) + unit * UNIT
+        start4 = jnp.where(row == column, 4.0, 0.0)
+        inverse = scale_c * (start4 - 6.0 * first.astype(jnp.float32) + 4.0 * second - third)
+        whole = cbuf[...].reshape(tokens, TILE)
+        return contract(whole, inverse.astype(jnp.bfloat16), 1, 0).astype(jnp.bfloat16)
+
+    def is_mine(k):
+        place = place_of(k)
+        return jnp.logical_and(place >= 0, place < 3)
+
+    def unit_step(k, carry):
+        value = unit_value(k)
+        inside = is_mine(k)
+
+        @pl.when(inside)
+        def _():
+            pre[:, strip_columns(place_of(k))] = value
+            pre_copy(place_of(k), pre_send.at[k], core_peer).start()
+
+        @pl.when(jnp.logical_not(inside))
+        def _():
+            give[...] = value
+            give_copy(k).start()
+
+        return carry
+
+    lax.fori_loop(0, 1 + edge, unit_step, 0)
+
+    row_slots = pl.ds(y * line * 2, line * 2)
+    row_tokens = pl.ds(pl.multiple_of(y * (tokens // 2), tokens // 2), tokens // 2)
+    row_n = nbuf[row_slots].reshape(tokens // 2, TILE)
+    gram_n[...] = contract(row_n, row_n, 0, 0)
+
+    def pre_flow(place, act):
+        unit = place + 3 * p - 4 * block
+        outside = jnp.logical_or(unit < 0, unit > 3)
+        source = jnp.where(edge == 1, unit // 2, unit - 2 * (r - 1))
+        gate = 2 - r
+        incoming = jnp.logical_or(outside, source != c)
+
+        @pl.when(incoming)
+        def _():
+            act(pre_copy(place, pre_send.at[3], core_peer), False)
+
+        @pl.when(jnp.logical_and(outside, gate == c))
+        def _():
+            act(pre_copy(place, pre_send.at[3], core_peer), True)
+
+    def pre_in(copy, forward):
+        if forward:
+            copy.start()
+        else:
+            copy.wait_recv()
+
+    def pre_done(copy, forward):
+        if forward:
+            copy.wait_send()
+
+    for place in range(3):
+        pre_flow(place, pre_in)
+
+    cross[...] = contract(pre[row_tokens, :], nbuf[row_slots].reshape(tokens // 2, TILE), 0, 0)
+
+    def other_row(i, carry):
+        zs, _ = line_source(jnp.maximum(i - 1, 0))
+        zs = jnp.where(i == 0, z, zs)
+        slot = slot_of(1 - y, zs, 0)
+        for cs in range(2):
+            n_to_y(slot + cs).wait_recv()
+        piece = nbuf[pl.ds(slot, 2)].reshape(2 * tokens_here, TILE)
+        gram_n[...] += contract(piece, piece, 0, 0)
+        rows = pl.ds(pl.multiple_of(slot * tokens_here, 2 * tokens_here), 2 * tokens_here)
+        cross[...] += contract(pre[rows, :], piece, 0, 0)
+        return carry
+
+    lax.fori_loop(0, line, other_row, 0)
+
+    scale_n = scaled_factor(gram_n, low_n, tokens)
+
+    def result(h):
+        rows = cross[pl.ds(pl.multiple_of(h * strip, strip), strip), :]
+        first = contract(rows.astype(jnp.bfloat16), low_n[...], 1, 0)
+        second = contract(first.astype(jnp.bfloat16), low_n[...], 1, 0)
+        third = contract(second.astype(jnp.bfloat16), low_n[...], 1, 0)
+        return scale_n * (4.0 * rows - 6.0 * first + 4.0 * second - third)
+
+    def energy(value):
+        total = jnp.sum((value * value).reshape(strip // 8, 8, TILE), axis=0)
+        part = total[:, :128]
+        for i in range(1, TILE // 128):
+            part = part + total[:, i * 128 : (i + 1) * 128]
+        return part
+
+    theirs[...] = result(1 - c)
+    swap = remote(theirs, arrived, swap_send.at[0], swap_recv.at[0], core_peer)
+    swap.start()
+    mine[...] = result(c)
+    squares[flat] = energy(theirs[...]) + energy(mine[...])
+
+    def sq_copy(d, slot):
+        target = (flat + d) % devices
+        return remote(
+            squares.at[slot],
+            squares.at[slot],
+            sq_send.at[d],
+            sq_recv.at[slot],
+            (target // owners, target % owners),
+        )
+
+    def sq_start(d, carry):
+        sq_copy(d, flat).start()
+        return carry
+
+    def sq_wait(d, carry):
+        sq_copy(d, (flat + d) % devices).wait_recv()
+        return carry
+
+    lax.fori_loop(1, devices, sq_start, 0)
+    lax.fori_loop(1, devices, sq_wait, 0)
+    total = jnp.sum(squares[...], axis=0)
+    total = jnp.sum(jnp.sum(total, axis=0, keepdims=True), axis=1, keepdims=True)
+    final = lax.rsqrt(total / (width * out_width) + 1e-06)
+    swap.wait_recv()
+    update_ref[:, pl.ds(pl.multiple_of(c * TILE, TILE), TILE)] = (mine[...] * final).astype(
+        jnp.bfloat16
+    )
+    update_ref[:, pl.ds(pl.multiple_of((1 - c) * TILE, TILE), TILE)] = (
+        arrived[...] * final
+    ).astype(jnp.bfloat16)
+
+    def sq_drain(d, carry):
+        sq_copy(d, flat).wait_send()
+        return carry
+
+    lax.fori_loop(1, devices, sq_drain, 0)
+    swap.wait_send()
+    n_pass.wait_send()
+    own_out(own_slot, drain)
+    own_out(core_slot, drain)
+
+    def line_drain(i, carry):
+        zs, below = line_source(i)
+        for cs in range(2):
+            line_out(slot_of(y, zs, cs), below, drain)
+        return carry
+
+    lax.fori_loop(0, line - 1, line_drain, 0)
+    c_own.wait_send()
+
+    def c_drain(k):
+        slot = c_in_slot(k, 0)
+        c_out(k).wait_send()
+        c_relay(slot, c_x, x_peer).wait_send()
+        c_relay(slot, c_core, core_peer).wait_send()
+
+    def c_shared_drain(k):
+        c_relay(c_in_slot(k, 1), c_core, core_peer).wait_send()
+
+    for k in range(1, line):
+        c_drain(k)
+        c_shared_drain(k)
+
+    @pl.when(x == 1)
+    def _():
+        c_drain(0)
+
+    @pl.when(x == 0)
+    def _():
+        c_shared_drain(0)
+
+    def unit_drain(k, carry):
+        inside = is_mine(k)
+
+        @pl.when(inside)
+        def _():
+            pre_copy(place_of(k), pre_send.at[k], core_peer).wait_send()
+
+        @pl.when(jnp.logical_not(inside))
+        def _():
+            give_copy(k).wait_send()
+
+        return carry
+
+    lax.fori_loop(0, 1 + edge, unit_drain, 0)
+    for place in range(3):
+        pre_flow(place, pre_done)
+
+
+def whole(groups, owners, hidden, norm_gain, cotangent):
+    tokens_here, width = hidden.shape
+    out_width = cotangent.shape[1]
+    tokens = groups * tokens_here
+    strip = out_width // groups
+    line = groups // 4
+    low, high = jnp.bfloat16, jnp.float32
+    dma = pltpu.SemaphoreType.DMA
+    return pl.pallas_call(
+        functools.partial(whole_kernel, (groups, owners, tokens_here, width, out_width)),
+        out_shape=jax.ShapeDtypeStruct((strip, width // owners), low),
+        in_specs=[
+            pl.BlockSpec(memory_space=pl.ANY),
+            pl.BlockSpec(memory_space=pltpu.VMEM),
+            pl.BlockSpec(memory_space=pl.ANY),
+        ],
+        out_specs=pl.BlockSpec(memory_space=pltpu.VMEM),
+        scratch_shapes=[
+            pltpu.VMEM((tokens_here, width), low),
+            pltpu.VMEM((groups, tokens_here, TILE), low),
+            pltpu.VMEM((groups, tokens_here, TILE), low),
+            pltpu.VMEM((tokens_here, TILE), low),
+            pltpu.VMEM((TILE, TILE), high),
+            pltpu.VMEM((TILE, TILE), high),
+            pltpu.VMEM((TILE, TILE), low),
+            pltpu.VMEM((TILE, TILE), low),
+            pltpu.VMEM((tokens, 2 * strip), low),
+            pltpu.VMEM((tokens, UNIT), low),
+            pltpu.VMEM((2 * strip, TILE), high),
+            pltpu.VMEM((strip, TILE), high),
+            pltpu.VMEM((strip, TILE), high),
+            pltpu.VMEM((strip, TILE), high),
+            pltpu.VMEM((groups * owners, 8, 128), high),
+            dma((2,)),
+            dma((line,)),
+            dma((groups,)),
+            dma((groups,)),
+            dma((groups,)),
+            dma((1,)),
+            dma((groups,)),
+            dma((groups,)),
+            dma((groups,)),
+            dma((groups,)),
+            dma((4,)),
+            dma((3,)),
+            dma((1,)),
+            dma((1,)),
+            dma((groups * owners,)),
+            dma((groups * owners,)),
+        ],
+        compiler_params=pltpu.CompilerParams(
+            collective_id=0, has_side_effects=True, vmem_limit_bytes=60 * 2**20
+        ),
+    )(hidden, norm_gain.reshape(1, width), cotangent)
+
+
+def fits(groups, owners, width, out_width):
+    line = groups // 4
+    return (
+        owners == 2
+        and width == 2 * owners * TILE
+        and groups % 8 == 0
+        and line & (line - 1) == 0
+        and line >= 4
+        and 8 * out_width == 3 * TILE * groups
+    )
+
+
+def step(hidden, norm_gain, cotangent):
+    groups, owners = lax.axis_size("dp"), lax.axis_size("owner")
+    if fits(groups, owners, hidden.shape[1], cotangent.shape[1]):
+        return whole(groups, owners, hidden, norm_gain, cotangent)
+    return shards(hidden, norm_gain, cotangent)
+
+
 def solution(mesh):
     in_specs = (P("dp", None), P(), P("dp", None))
     out_specs = P("dp", "owner")
-    return jax.shard_map(shards, mesh=mesh, in_specs=in_specs, out_specs=out_specs, check_vma=False)
+    return jax.shard_map(step, mesh=mesh, in_specs=in_specs, out_specs=out_specs, check_vma=False)

time: 328 us -> 116 us (0.35); the launches traced: 322 us -> 116 us
  Pallas kernels: 0 us -> 113 us
  waiting for transfers between devices: 91.5 us -> 0 us
  matrix products: 84.1 us -> 0 us
  blocking collectives: 54.5 us -> 0 us
  local copies, waits for them, and re-layouts: 43.5 us -> 2.73 us
  between operations: 27.3 us -> 0.01 us
  other arithmetic: 11.9 us -> 0 us
  starting transfers between devices: 9.01 us -> 0 us
    pallas_call x0 -> x1, Pallas kernels: none -> 113 us  [whole(): pl.pallas_call(functools.partial(whole_kernel, (groups, owners, tokens_he...]
    all_to_all x1 -> x0, waiting for transfers between devices: 91.5 us -> none  [shards(): lax.all_to_all(outgoing, 'dp', 0, 0, tiled=True).reshape(tokens, TILE)]
    dot_general x9 -> x0, matrix products: 84.1 us -> none  [contract(): lax.dot_general(left, right, (((left_dim,), (right_dim,)), ((), ())), pre...]
    psum x1 -> x0, blocking collectives: 54.5 us -> none  [shards(): squares = lax.psum(jnp.sum(summed * summed), ('dp', 'owner'))]
    dynamic_slice x19 -> x0, local copies, waits for them, and re-layouts: 19.5 us -> none  [the longest x17 18.8 us: shards(): lax.dynamic_slice_in_dim(cotangent, wanted[g] * TILE, TILE, 1)]
    unnamed x35 -> x1, local copies, waits for them, and re-layouts: 16.7 us -> 2.73 us
    all_to_all x1 -> x0, starting transfers between devices: 7.47 us -> none  [shards(): lax.all_to_all(outgoing, 'dp', 0, 0, tiled=True).reshape(tokens, TILE)]
    all_to_all x1 -> x0, local copies, waits for them, and re-layouts: 6.56 us -> none  [shards(): lax.all_to_all(outgoing, 'dp', 0, 0, tiled=True).reshape(tokens, TILE)]
  transfers between devices with their start and end apart: 3 -> 0, of which waited for: 1 -> 0; matrix products, arithmetic and copies ran while one was open for 37% -> 0% of each run, Pallas kernels for 0% -> 0%
where the time goes in v1:
time: 116 us
  Pallas kernels  113 us (97%)
  local copies, waits for them, and re-layouts  2.73 us (2%)
    pallas_call x1, Pallas kernels, whole(): pl.pallas_call(functools.partial(whole_kernel, (groups, owners, tokens_he...  113 us
    unnamed x1, local copies, waits for them, and re-layouts  2.73 us

profile of v1, /device:TPU:0, one launch (start us, length us, event | category | flops | bytes accessed | tf_op | source)
XLA Modules:
  0.0 115.7 jit_solution(8381909475780879784)
XLA Ops:
  0.0 113.0 %shard_map.37 = bf16[384,2048]{1,0:T(8,128)(2,1)} custom-call(bf16[128,4096]{1,0:T(8,128)(2,1)} %hidden_ref.1, f32[1,4096]{1,0:T(1,128)} %bitcast.1, bf16[128,6144]{1,0:T(8,128)(2,1)} %cotangent_ref.1), custom_call_target="tpu_custom_call" | custom-call | tf_op jit(solution)/shard_map/pallas_call | solution.py:604
  113.0 2.7 %copy.5 = bf16[384,2048]{1,0:T(8,128)(2,1)} copy(bf16[384,2048]{1,0:T(8,128)(2,1)} %shard_map.37) | data formatting | bytes 3145728

commit v2 on v1

--- a/solution.py
+++ b/solution.py
@@ -88,6 +88,23 @@
 MESH = pl.DeviceIdType.MESH
 UNIT = TILE // 4
 CHUNK = 128
+EARLY = (1, 2, 3)
+MIDDLE = (
+    ("d0", "d2", "d1", "s2", "L10", "s0", "d3", "L00", "s1", "L11", "L01", "s3",),
+    (),
+    ("L20", "S0",),
+    ("L21",),
+    (),
+    ("Y", "S1", "P", "S2",),
+)
+END = (
+    ("d1", "S2", "d2", "s1", "d0", "S0", "Y", "s0", "d3", "L00", "s3", "L01", "s2",),
+    ("L10",),
+    (),
+    ("S1", "L20",),
+    ("P", "L11", "L21",),
+    (),
+)
 
 
 def flipped(value, mask):
@@ -138,10 +155,12 @@
     pre,
     give,
     cross,
+    second_low,
     mine,
     theirs,
     arrived,
     squares,
+    meet,
     load_sem,
     c_send,
     c_x,
@@ -201,15 +220,25 @@
 
     barrier = pltpu.get_barrier_semaphore()
 
-    def greet(d, carry):
-        target = (flat + d) % devices
-        pl.semaphore_signal(
-            barrier, inc=1, device_id=(target // owners, target % owners), device_id_type=MESH
-        )
-        return carry
-
-    lax.fori_loop(1, devices, greet, 0)
-    pl.semaphore_wait(barrier, devices - 1)
+    def greet(target):
+        pl.semaphore_signal(barrier, inc=1, device_id=target, device_id_type=MESH)
+
+    greet(core_peer)
+    greet(x_peer)
+    greet(device(x, 1 - y, z, c))
+    for k in range(1, line):
+        zd = flipped(z, k)
+        greet(device(x, (y + x + z + zd) % 2, zd, c))
+
+    @pl.when(z + 1 < line)
+    def _():
+        greet(device(x, y, z + 1, c))
+
+    @pl.when(z > 0)
+    def _():
+        greet(device(x, y, z - 1, c))
+
+    pl.semaphore_wait(barrier, 2 + line + jnp.where(z + 1 < line, 1, 0) + jnp.where(z > 0, 1, 0))
 
     def block_columns(y_, z_):
         return pl.ds(pl.multiple_of(block_of(z_ * 2 + y_) * TILE, TILE), TILE)
@@ -233,7 +262,8 @@
     def c_relay(slot, sems, target):
         return remote(cbuf.at[slot], cbuf.at[slot], sems.at[slot], c_recv.at[slot], target)
 
-    for k in range(1, line):
+    early = EARLY
+    for k in early:
         c_out(k).start()
 
     @pl.when(x == 1)
@@ -303,6 +333,9 @@
     own_out(own_slot, start)
     n_to_y(core_slot).wait_recv()
     own_out(core_slot, start)
+    for k in range(1, line):
+        if k not in early:
+            c_out(k).start()
 
     def line_source(i):
         low = jnp.minimum(z, line - 1 - z)
@@ -312,8 +345,6 @@
         return jnp.where(below, z - distance, z + distance), below
 
     def line_out(slot, below, act):
-        act(n_to_y(slot))
-
         @pl.when(jnp.logical_and(below, z + 1 < line))
         def _():
             act(n_to_up(slot))
@@ -322,13 +353,42 @@
         def _():
             act(n_to_down(slot))
 
-    def line_step(i, carry):
+    is_end = jnp.logical_or(z == 0, z == line - 1)
+
+    def from_end(zs):
+        return jnp.logical_or(zs == 0, zs == line - 1)
+
+    def line_piece(i, cs, act, wait):
         zs, below = line_source(i)
-        for cs in range(2):
-            slot = slot_of(y, zs, cs)
+        slot = slot_of(y, zs, cs)
+        if wait:
             n_to_y(slot).wait_recv()
-            line_out(slot, below, start)
-        return carry
+        line_out(slot, below, act)
+        if cs == 0:
+
+            @pl.when(jnp.logical_not(from_end(zs)))
+            def _():
+                act(n_to_y(slot))
+        else:
+            act(n_to_y(slot))
+
+    def crossed_piece(i, act, wait):
+        zs, below = line_source(i)
+
+        @pl.when(jnp.logical_and(from_end(zs), jnp.logical_not(is_end)))
+        def _():
+            slot = slot_of(1 - y, zs, 0)
+            if wait:
+                n_to_y(slot).wait_recv()
+            line_out(slot, below, act)
+
+    def crossed_here(act, wait):
+        @pl.when(is_end)
+        def _():
+            slot = slot_of(1 - y, z, 0)
+            if wait:
+                n_to_y(slot).wait_recv()
+            line_out(slot, z == 0, act)
 
     def c_direct(k):
         slot = c_in_slot(k, 0)
@@ -336,40 +396,30 @@
         c_relay(slot, c_x, x_peer).start()
         c_relay(slot, c_core, core_peer).start()
 
-    for k in range(1, line):
-        c_direct(k)
-
-    @pl.when(x == 1)
-    def _():
-        c_direct(0)
-
-    line_step(0, 0)
+    def c_from_core(i, carry):
+        slot = 2 * i + 1 - c
+        c_relay(slot, c_core, core_peer).wait_recv()
+        return carry
+
+    def direct_zero():
+        @pl.when(x == 1)
+        def _():
+            c_direct(0)
 
     def c_shared(k):
         slot = c_in_slot(k, 1)
         c_relay(slot, c_core, core_peer).wait_recv()
         c_relay(slot, c_core, core_peer).start()
 
-    for k in range(1, line):
-        c_shared(k)
-
-    @pl.when(x == 0)
-    def _():
-        c_shared(0)
-
-    def c_from_core(i, carry):
-        slot = 2 * i + 1 - c
-        c_relay(slot, c_core, core_peer).wait_recv()
-        return carry
-
-    lax.fori_loop(0, groups // 2, c_from_core, 0)
-    local.wait()
-
-    line_step(1, 0)
-    block_tokens = cbuf[...].reshape(tokens, TILE)
-    gram_c[...] = contract(block_tokens, block_tokens, 0, 0)
-    scale_c = scaled_factor(gram_c, low_c, tokens)
-    lax.fori_loop(2, line - 1, line_step, 0)
+    def shared_zero():
+        @pl.when(x == 0)
+        def _():
+            c_shared(0)
+
+    def gram_rows(i):
+        block_tokens = cbuf[...].reshape(tokens, TILE)
+        part = slice(i * TILE // 2, (i + 1) * TILE // 2)
+        gram_c[part, :] = contract(block_tokens[:, part], block_tokens, 0, 0)
 
     p = z * 2 + y
     r = p % 4
@@ -389,17 +439,53 @@
         view = pre.at[:, strip_columns(place)]
         return remote(view, view, send, pre_recv.at[place], target)
 
-    def give_copy(k):
-        place = place_of(k) - 3 * (1 - 2 * y)
+    half = tokens // 2
+
+    def half_rows(h):
+        return pl.ds(pl.multiple_of(h * half, half), half)
+
+    def give_copy():
+        place = place_of(0) - 3 * (1 - 2 * y)
         return remote(
             give,
-            pre.at[:, strip_columns(place)],
+            pre.at[half_rows(x), strip_columns(place)],
             pre_send.at[2],
-            pre_recv.at[place],
+            pre_recv.at[3 + x],
             device(x, 1 - y, z, c),
         )
 
-    def unit_value(k):
+    outer_place = (r - 1) * 2
+
+    def outer_copy(h, send, target):
+        view = pre.at[half_rows(h), strip_columns(outer_place)]
+        return remote(view, view, pre_send.at[send], pre_recv.at[3 + h], target)
+
+    def outer_first():
+        @pl.when(jnp.logical_and(edge == 0, c == 2 - r))
+        def _():
+            outer_copy(x, 3, x_peer).wait_recv()
+            outer_copy(x, 3, x_peer).start()
+            outer_copy(x, 4, core_peer).start()
+
+    def outer_rest():
+        @pl.when(jnp.logical_and(edge == 0, c == 2 - r))
+        def _():
+            outer_copy(1 - x, 5, core_peer).wait_recv()
+            outer_copy(1 - x, 5, core_peer).start()
+
+        @pl.when(jnp.logical_and(edge == 0, c == r - 1))
+        def _():
+            outer_copy(0, 3, core_peer).wait_recv()
+            outer_copy(1, 3, core_peer).wait_recv()
+
+    def outer_drain():
+        @pl.when(jnp.logical_and(edge == 0, c == 2 - r))
+        def _():
+            outer_copy(x, 3, x_peer).wait_send()
+            outer_copy(x, 4, core_peer).wait_send()
+            outer_copy(1 - x, 5, core_peer).wait_send()
+
+    def unit_inverse(k, scale_c):
         unit = unit_of(k)
         first = low_c[:, pl.ds(pl.multiple_of(unit * UNIT, UNIT), UNIT)]
         second = contract(low_c[...], first, 1, 0)
@@ -408,63 +494,105 @@
         column = lax.broadcasted_iota(jnp.int32, (TILE, UNIT), 1) + unit * UNIT
         start4 = jnp.where(row == column, 4.0, 0.0)
         inverse = scale_c * (start4 - 6.0 * first.astype(jnp.float32) + 4.0 * second - third)
-        whole = cbuf[...].reshape(tokens, TILE)
-        return contract(whole, inverse.astype(jnp.bfloat16), 1, 0).astype(jnp.bfloat16)
+        return inverse.astype(jnp.bfloat16)
 
     def is_mine(k):
         place = place_of(k)
         return jnp.logical_and(place >= 0, place < 3)
 
-    def unit_step(k, carry):
-        value = unit_value(k)
+    def unit_step(k, scale_c):
+        inverse = unit_inverse(k, scale_c)
         inside = is_mine(k)
 
         @pl.when(inside)
         def _():
-            pre[:, strip_columns(place_of(k))] = value
+            whole = cbuf[...].reshape(tokens, TILE)
+            pre[:, strip_columns(place_of(k))] = contract(whole, inverse, 1, 0).astype(jnp.bfloat16)
             pre_copy(place_of(k), pre_send.at[k], core_peer).start()
 
         @pl.when(jnp.logical_not(inside))
         def _():
-            give[...] = value
-            give_copy(k).start()
-
-        return carry
-
-    lax.fori_loop(0, 1 + edge, unit_step, 0)
+            rows = cbuf[pl.ds(x * (groups // 2), groups // 2)].reshape(half, TILE)
+            give[...] = contract(rows, inverse, 1, 0).astype(jnp.bfloat16)
+            give_copy().start()
 
     row_slots = pl.ds(y * line * 2, line * 2)
     row_tokens = pl.ds(pl.multiple_of(y * (tokens // 2), tokens // 2), tokens // 2)
+
+    def move(token):
+        kind = token[0]
+        if kind == "d":
+            k = int(token[1])
+            if k:
+                c_direct(k)
+            else:
+                direct_zero()
+        elif kind == "s":
+            k = int(token[1])
+            if k:
+                c_shared(k)
+            else:
+                shared_zero()
+        elif kind == "L":
+            line_piece(int(token[1]), int(token[2]), start, True)
+        elif kind == "S":
+            crossed_piece(int(token[1]), start, True)
+        elif kind == "Y":
+            crossed_here(start, True)
+        elif kind == "P":
+            outer_first()
+
+    def moves(stage):
+        @pl.when(is_end)
+        def _():
+            for token in END[stage]:
+                move(token)
+
+        @pl.when(jnp.logical_not(is_end))
+        def _():
+            for token in MIDDLE[stage]:
+                move(token)
+
+    moves(0)
+    lax.fori_loop(0, groups // 2, c_from_core, 0)
+    local.wait()
+    gram_rows(0)
+    moves(1)
+    gram_rows(1)
+    scale_c = scaled_factor(gram_c, low_c, tokens)
+    moves(2)
+    unit_step(0, scale_c)
+    moves(3)
+
+    @pl.when(edge == 1)
+    def _():
+        unit_step(1, scale_c)
+
+    moves(4)
+
+    def more(i, carry):
+        for cs in range(2):
+            line_piece(i, cs, start, True)
+        crossed_piece(i, start, True)
+        return carry
+
+    lax.fori_loop(3, line - 1, more, 0)
     row_n = nbuf[row_slots].reshape(tokens // 2, TILE)
     gram_n[...] = contract(row_n, row_n, 0, 0)
-
-    def pre_flow(place, act):
+    moves(5)
+
+    def pre_in(place):
         unit = place + 3 * p - 4 * block
-        outside = jnp.logical_or(unit < 0, unit > 3)
+        inside = jnp.logical_and(unit >= 0, unit <= 3)
         source = jnp.where(edge == 1, unit // 2, unit - 2 * (r - 1))
-        gate = 2 - r
-        incoming = jnp.logical_or(outside, source != c)
-
-        @pl.when(incoming)
-        def _():
-            act(pre_copy(place, pre_send.at[3], core_peer), False)
-
-        @pl.when(jnp.logical_and(outside, gate == c))
-        def _():
-            act(pre_copy(place, pre_send.at[3], core_peer), True)
-
-    def pre_in(copy, forward):
-        if forward:
-            copy.start()
-        else:
-            copy.wait_recv()
-
-    def pre_done(copy, forward):
-        if forward:
-            copy.wait_send()
+
+        @pl.when(jnp.logical_and(inside, source != c))
+        def _():
+            pre_copy(place, pre_send.at[0], core_peer).wait_recv()
 
     for place in range(3):
-        pre_flow(place, pre_in)
+        pre_in(place)
+    outer_rest()
 
     cross[...] = contract(pre[row_tokens, :], nbuf[row_slots].reshape(tokens // 2, TILE), 0, 0)
 
@@ -472,8 +600,14 @@
         zs, _ = line_source(jnp.maximum(i - 1, 0))
         zs = jnp.where(i == 0, z, zs)
         slot = slot_of(1 - y, zs, 0)
-        for cs in range(2):
-            n_to_y(slot + cs).wait_recv()
+
+        seen = jnp.where(i == 0, is_end, jnp.logical_and(from_end(zs), jnp.logical_not(is_end)))
+
+        @pl.when(jnp.logical_not(seen))
+        def _():
+            n_to_y(slot).wait_recv()
+
+        n_to_y(slot + 1).wait_recv()
         piece = nbuf[pl.ds(slot, 2)].reshape(2 * tokens_here, TILE)
         gram_n[...] += contract(piece, piece, 0, 0)
         rows = pl.ds(pl.multiple_of(slot * tokens_here, 2 * tokens_here), 2 * tokens_here)
@@ -482,14 +616,19 @@
 
     lax.fori_loop(0, line, other_row, 0)
 
+    pl.semaphore_signal(meet, inc=1, device_id=x_peer, device_id_type=MESH)
     scale_n = scaled_factor(gram_n, low_n, tokens)
 
+    first = contract(cross[...].astype(jnp.bfloat16), low_n[...], 1, 0)
+    cross[...] = 4.0 * cross[...] - 6.0 * first
+    second = contract(first.astype(jnp.bfloat16), low_n[...], 1, 0)
+    cross[...] += 4.0 * second
+    second_low[...] = second.astype(jnp.bfloat16)
+
     def result(h):
-        rows = cross[pl.ds(pl.multiple_of(h * strip, strip), strip), :]
-        first = contract(rows.astype(jnp.bfloat16), low_n[...], 1, 0)
-        second = contract(first.astype(jnp.bfloat16), low_n[...], 1, 0)
-        third = contract(second.astype(jnp.bfloat16), low_n[...], 1, 0)
-        return scale_n * (4.0 * rows - 6.0 * first + 4.0 * second - third)
+        rows = pl.ds(pl.multiple_of(h * strip, strip), strip)
+        third = contract(second_low[rows, :], low_n[...], 1, 0)
+        return scale_n * (cross[rows, :] - third)
 
     def energy(value):
         total = jnp.sum((value * value).reshape(strip // 8, 8, TILE), axis=0)
@@ -522,15 +661,16 @@
         sq_copy(d, (flat + d) % devices).wait_recv()
         return carry
 
+    pl.semaphore_wait(meet, 1)
     lax.fori_loop(1, devices, sq_start, 0)
     lax.fori_loop(1, devices, sq_wait, 0)
     total = jnp.sum(squares[...], axis=0)
     total = jnp.sum(jnp.sum(total, axis=0, keepdims=True), axis=1, keepdims=True)
     final = lax.rsqrt(total / (width * out_width) + 1e-06)
-    swap.wait_recv()
     update_ref[:, pl.ds(pl.multiple_of(c * TILE, TILE), TILE)] = (mine[...] * final).astype(
         jnp.bfloat16
     )
+    swap.wait_recv()
     update_ref[:, pl.ds(pl.multiple_of((1 - c) * TILE, TILE), TILE)] = (
         arrived[...] * final
     ).astype(jnp.bfloat16)
@@ -546,12 +686,13 @@
     own_out(core_slot, drain)
 
     def line_drain(i, carry):
-        zs, below = line_source(i)
         for cs in range(2):
-            line_out(slot_of(y, zs, cs), below, drain)
+            line_piece(i, cs, drain, False)
+        crossed_piece(i, drain, False)
         return carry
 
     lax.fori_loop(0, line - 1, line_drain, 0)
+    crossed_here(drain, False)
     c_own.wait_send()
 
     def c_drain(k):
@@ -584,13 +725,12 @@
 
         @pl.when(jnp.logical_not(inside))
         def _():
-            give_copy(k).wait_send()
+            give_copy().wait_send()
 
         return carry
 
     lax.fori_loop(0, 1 + edge, unit_drain, 0)
-    for place in range(3):
-        pre_flow(place, pre_done)
+    outer_drain()
 
 
 def whole(groups, owners, hidden, norm_gain, cotangent):
@@ -620,12 +760,14 @@
             pltpu.VMEM((TILE, TILE), low),
             pltpu.VMEM((TILE, TILE), low),
             pltpu.VMEM((tokens, 2 * strip), low),
-            pltpu.VMEM((tokens, UNIT), low),
+            pltpu.VMEM((tokens // 2, UNIT), low),
             pltpu.VMEM((2 * strip, TILE), high),
+            pltpu.VMEM((2 * strip, TILE), low),
             pltpu.VMEM((strip, TILE), high),
             pltpu.VMEM((strip, TILE), high),
             pltpu.VMEM((strip, TILE), high),
             pltpu.VMEM((groups * owners, 8, 128), high),
+            pltpu.SemaphoreType.REGULAR,
             dma((2,)),
             dma((line,)),
             dma((groups,)),
@@ -636,8 +778,8 @@
             dma((groups,)),
             dma((groups,)),
             dma((groups,)),
-            dma((4,)),
-            dma((3,)),
+            dma((6,)),
+            dma((5,)),
             dma((1,)),
             dma((1,)),
             dma((groups * owners,)),

time: 116 us -> 101 us (0.87)
  Pallas kernels: 113 us -> 97.6 us
    pallas_call x1, Pallas kernels: 113 us -> 97.6 us  [whole(): pl.pallas_call(functools.partial(whole_kernel, (groups, owners, tokens_he...]
where the time goes in v2:
time: 101 us; the launch traced here: 100 us
  Pallas kernels  97.6 us (97%)
  local copies, waits for them, and re-layouts  2.73 us (3%)
    pallas_call x1, Pallas kernels, whole(): pl.pallas_call(functools.partial(whole_kernel, (groups, owners, tokens_he...  97.6 us
    unnamed x1, local copies, waits for them, and re-layouts  2.73 us

profile of v2, /device:TPU:0, one launch (start us, length us, event | category | flops | bytes accessed | tf_op | source)
XLA Modules:
  0.0 100.3 jit_solution(11601346232820275616)
XLA Ops:
  0.0 97.6 %shard_map.37 = bf16[384,2048]{1,0:T(8,128)(2,1)} custom-call(bf16[128,4096]{1,0:T(8,128)(2,1)} %hidden_ref.1, f32[1,4096]{1,0:T(1,128)} %bitcast.1, bf16[128,6144]{1,0:T(8,128)(2,1)} %cotangent_ref.1), custom_call_target="tpu_custom_call" | custom-call | tf_op jit(solution)/shard_map/pallas_call | solution.py:744
  97.6 2.7 %copy.5 = bf16[384,2048]{1,0:T(8,128)(2,1)} copy(bf16[384,2048]{1,0:T(8,128)(2,1)} %shard_map.37) | data formatting | bytes 3145728

commit v3 on v2

--- a/solution.py
+++ b/solution.py
@@ -114,28 +114,22 @@
     return value
 
 
-def matrix_chunk(gram, tokens, i):
-    shape = (CHUNK, TILE)
-    row = lax.broadcasted_iota(jnp.int32, shape, 0) + i * CHUNK
-    column = lax.broadcasted_iota(jnp.int32, shape, 1)
-    rows = pl.ds(pl.multiple_of(i * CHUNK, CHUNK), CHUNK)
-    return gram[rows, :] * (1.0 / tokens) + jnp.where(row == column, DAMPING, 0.0)
-
-
-def scaled_factor(gram, low, tokens):
-    def add(i, total):
-        return total + jnp.sum(jnp.abs(matrix_chunk(gram, tokens, i)), axis=0, keepdims=True)
-
-    sums = lax.fori_loop(0, TILE // CHUNK, add, jnp.zeros((1, TILE), jnp.float32))
-    scale = 1.0 / jnp.max(sums, axis=1, keepdims=True)
-
-    def put(i, carry):
+def rounded_factor(gram, low, tokens):
+    row = lax.broadcasted_iota(jnp.int32, (CHUNK, CHUNK), 0)
+    column = lax.broadcasted_iota(jnp.int32, (CHUNK, CHUNK), 1)
+    damping = jnp.where(row == column, DAMPING, 0.0)
+
+    def put(i, total):
         rows = pl.ds(pl.multiple_of(i * CHUNK, CHUNK), CHUNK)
-        low[rows, :] = (scale * matrix_chunk(gram, tokens, i)).astype(jnp.bfloat16)
-        return carry
-
-    lax.fori_loop(0, TILE // CHUNK, put, 0)
-    return scale
+        matrix = gram[rows, :] * (1.0 / tokens)
+        low[rows, :] = matrix.astype(jnp.bfloat16)
+        low[rows, rows] = (gram[rows, rows] * (1.0 / tokens) + damping).astype(jnp.bfloat16)
+        folded = jnp.sum(jnp.abs(matrix).reshape(CHUNK // 8, 8, TILE), axis=0)
+        return total + folded
+
+    sums = lax.fori_loop(0, TILE // CHUNK, put, jnp.zeros((8, TILE), jnp.float32))
+    sums = jnp.sum(sums, axis=0, keepdims=True)
+    return 1.0 / (jnp.max(sums, axis=1, keepdims=True) + DAMPING)
 
 
 def whole_kernel(
@@ -493,7 +487,9 @@
         row = lax.broadcasted_iota(jnp.int32, (TILE, UNIT), 0)
         column = lax.broadcasted_iota(jnp.int32, (TILE, UNIT), 1) + unit * UNIT
         start4 = jnp.where(row == column, 4.0, 0.0)
-        inverse = scale_c * (start4 - 6.0 * first.astype(jnp.float32) + 4.0 * second - third)
+        powers = [scale_c, scale_c**2, scale_c**3, scale_c**4]
+        inverse = powers[0] * start4 - (6.0 * powers[1]) * first.astype(jnp.float32)
+        inverse = inverse + (4.0 * powers[2]) * second - powers[3] * third
         return inverse.astype(jnp.bfloat16)
 
     def is_mine(k):
@@ -559,7 +555,7 @@
     gram_rows(0)
     moves(1)
     gram_rows(1)
-    scale_c = scaled_factor(gram_c, low_c, tokens)
+    scale_c = rounded_factor(gram_c, low_c, tokens)
     moves(2)
     unit_step(0, scale_c)
     moves(3)
@@ -617,18 +613,19 @@
     lax.fori_loop(0, line, other_row, 0)
 
     pl.semaphore_signal(meet, inc=1, device_id=x_peer, device_id_type=MESH)
-    scale_n = scaled_factor(gram_n, low_n, tokens)
+    scale_n = rounded_factor(gram_n, low_n, tokens)
 
     first = contract(cross[...].astype(jnp.bfloat16), low_n[...], 1, 0)
-    cross[...] = 4.0 * cross[...] - 6.0 * first
+    square = scale_n * scale_n
+    cross[...] = (4.0 * scale_n) * cross[...] - (6.0 * square) * first
     second = contract(first.astype(jnp.bfloat16), low_n[...], 1, 0)
-    cross[...] += 4.0 * second
+    cross[...] += (4.0 * square * scale_n) * second
     second_low[...] = second.astype(jnp.bfloat16)
 
     def result(h):
         rows = pl.ds(pl.multiple_of(h * strip, strip), strip)
         third = contract(second_low[rows, :], low_n[...], 1, 0)
-        return scale_n * (cross[rows, :] - third)
+        return cross[rows, :] - (square * square) * third
 
     def energy(value):
         total = jnp.sum((value * value).reshape(strip // 8, 8, TILE), axis=0)

time: 101 us -> 97.4 us (0.964)
  Pallas kernels: 97.6 us -> 94.4 us
    pallas_call x1, Pallas kernels: 97.6 us -> 94.4 us  [whole(): pl.pallas_call(functools.partial(whole_kernel, (groups, owners, tokens_he...]
where the time goes in v3:
time: 97.4 us; the launch traced here: 97.1 us
  Pallas kernels  94.4 us (97%)
  local copies, waits for them, and re-layouts  2.73 us (3%)
    pallas_call x1, Pallas kernels, whole(): pl.pallas_call(functools.partial(whole_kernel, (groups, owners, tokens_he...  94.4 us
    unnamed x1, local copies, waits for them, and re-layouts  2.73 us

profile of v3, /device:TPU:0, one launch (start us, length us, event | category | flops | bytes accessed | tf_op | source)
XLA Modules:
  0.0 97.1 jit_solution(10176367139446673150)
XLA Ops:
  0.0 94.4 %shard_map.37 = bf16[384,2048]{1,0:T(8,128)(2,1)} custom-call(bf16[128,4096]{1,0:T(8,128)(2,1)} %hidden_ref.1, f32[1,4096]{1,0:T(1,128)} %bitcast.1, bf16[128,6144]{1,0:T(8,128)(2,1)} %cotangent_ref.1), custom_call_target="tpu_custom_call" | custom-call | tf_op jit(solution)/shard_map/pallas_call | solution.py:741
  94.4 2.7 %copy.5 = bf16[384,2048]{1,0:T(8,128)(2,1)} copy(bf16[384,2048]{1,0:T(8,128)(2,1)} %shard_map.37) | data formatting | bytes 3145728

commit v4 on v3

--- a/solution.py
+++ b/solution.py
@@ -98,7 +98,7 @@
     ("Y", "S1", "P", "S2",),
 )
 END = (
-    ("d1", "S2", "d2", "s1", "d0", "S0", "Y", "s0", "d3", "L00", "s3", "L01", "s2",),
+    ("d1", "S2", "s1", "s0", "d0", "S0", "d2", "Y", "d3", "L00", "s3", "L01", "s2",),
     ("L10",),
     (),
     ("S1", "L20",),
@@ -149,11 +149,14 @@
     pre,
     give,
     cross,
+    first_low,
     second_low,
     mine,
     theirs,
     arrived,
     squares,
+    put_low,
+    put_sem,
     meet,
     load_sem,
     c_send,
@@ -615,17 +618,18 @@
     pl.semaphore_signal(meet, inc=1, device_id=x_peer, device_id_type=MESH)
     scale_n = rounded_factor(gram_n, low_n, tokens)
 
+    square = scale_n * scale_n
     first = contract(cross[...].astype(jnp.bfloat16), low_n[...], 1, 0)
-    square = scale_n * scale_n
+    first_low[...] = first.astype(jnp.bfloat16)
     cross[...] = (4.0 * scale_n) * cross[...] - (6.0 * square) * first
-    second = contract(first.astype(jnp.bfloat16), low_n[...], 1, 0)
-    cross[...] += (4.0 * square * scale_n) * second
-    second_low[...] = second.astype(jnp.bfloat16)
+    second_low[...] = contract(first_low[...], low_n[...], 1, 0).astype(jnp.bfloat16)
 
     def result(h):
         rows = pl.ds(pl.multiple_of(h * strip, strip), strip)
-        third = contract(second_low[rows, :], low_n[...], 1, 0)
-        return cross[rows, :] - (square * square) * third
+        second = second_low[rows, :]
+        third = contract(second, low_n[...], 1, 0)
+        partial = cross[rows, :] + (4.0 * square * scale_n) * second.astype(jnp.float32)
+        return partial - (square * square) * third
 
     def energy(value):
         total = jnp.sum((value * value).reshape(strip // 8, 8, TILE), axis=0)
@@ -656,28 +660,11 @@
 
     def sq_wait(d, carry):
         sq_copy(d, (flat + d) % devices).wait_recv()
+        sq_copy(d, flat).wait_send()
         return carry
 
     pl.semaphore_wait(meet, 1)
     lax.fori_loop(1, devices, sq_start, 0)
-    lax.fori_loop(1, devices, sq_wait, 0)
-    total = jnp.sum(squares[...], axis=0)
-    total = jnp.sum(jnp.sum(total, axis=0, keepdims=True), axis=1, keepdims=True)
-    final = lax.rsqrt(total / (width * out_width) + 1e-06)
-    update_ref[:, pl.ds(pl.multiple_of(c * TILE, TILE), TILE)] = (mine[...] * final).astype(
-        jnp.bfloat16
-    )
-    swap.wait_recv()
-    update_ref[:, pl.ds(pl.multiple_of((1 - c) * TILE, TILE), TILE)] = (
-        arrived[...] * final
-    ).astype(jnp.bfloat16)
-
-    def sq_drain(d, carry):
-        sq_copy(d, flat).wait_send()
-        return carry
-
-    lax.fori_loop(1, devices, sq_drain, 0)
-    swap.wait_send()
     n_pass.wait_send()
     own_out(own_slot, drain)
     own_out(core_slot, drain)
@@ -728,6 +715,25 @@
 
     lax.fori_loop(0, 1 + edge, unit_drain, 0)
     outer_drain()
+    swap.wait()
+    lax.fori_loop(1, devices, sq_wait, 0)
+    total = jnp.sum(squares[...], axis=0)
+    total = jnp.sum(jnp.sum(total, axis=0, keepdims=True), axis=1, keepdims=True)
+    final = lax.rsqrt(total / (width * out_width) + 1e-06)
+
+    def put(half, value, h):
+        put_low[half] = (value * final).astype(jnp.bfloat16)
+        columns = pl.ds(pl.multiple_of(h * TILE, TILE), TILE)
+        copy = pltpu.make_async_copy(
+            put_low.at[half], update_ref.at[:, columns], put_sem.at[half]
+        )
+        copy.start()
+        return copy
+
+    first_put = put(0, mine[...], c)
+    second_put = put(1, arrived[...], 1 - c)
+    first_put.wait()
+    second_put.wait()
 
 
 def whole(groups, owners, hidden, norm_gain, cotangent):
@@ -746,7 +752,7 @@
             pl.BlockSpec(memory_space=pltpu.VMEM),
             pl.BlockSpec(memory_space=pl.ANY),
         ],
-        out_specs=pl.BlockSpec(memory_space=pltpu.VMEM),
+        out_specs=pl.BlockSpec(memory_space=pl.ANY),
         scratch_shapes=[
             pltpu.VMEM((tokens_here, width), low),
             pltpu.VMEM((groups, tokens_here, TILE), low),
@@ -760,10 +766,13 @@
             pltpu.VMEM((tokens // 2, UNIT), low),
             pltpu.VMEM((2 * strip, TILE), high),
             pltpu.VMEM((2 * strip, TILE), low),
+            pltpu.VMEM((2 * strip, TILE), low),
             pltpu.VMEM((strip, TILE), high),
             pltpu.VMEM((strip, TILE), high),
             pltpu.VMEM((strip, TILE), high),
             pltpu.VMEM((groups * owners, 8, 128), high),
+            pltpu.VMEM((2, strip, TILE), low),
+            dma((2,)),
             pltpu.SemaphoreType.REGULAR,
             dma((2,)),
             dma((line,)),

time: 97.4 us -> 96.9 us (level)
  no operation moved by 1% of the time
where the time goes in v4:
time: 96.9 us; the launch traced here: 96.6 us
  Pallas kernels  93.9 us (97%)
  local copies, waits for them, and re-layouts  2.73 us (3%)
    pallas_call x1, Pallas kernels, whole(): pl.pallas_call(functools.partial(whole_kernel, (groups, owners, tokens_he...  93.9 us
    unnamed x1, local copies, waits for them, and re-layouts  2.73 us

profile of v4, /device:TPU:0, one launch (start us, length us, event | category | flops | bytes accessed | tf_op | source)
XLA Modules:
  0.0 96.6 jit_solution(11376743719859975307)
XLA Ops:
  0.0 93.9 %shard_map.37 = bf16[384,2048]{1,0:T(8,128)(2,1)} custom-call(bf16[128,4096]{1,0:T(8,128)(2,1)} %hidden_ref.1, f32[1,4096]{1,0:T(1,128)} %bitcast.1, bf16[128,6144]{1,0:T(8,128)(2,1)} %cotangent_ref.1), custom_call_target="tpu_custom_call" | custom-call | tf_op jit(solution)/shard_map/pallas_call | solution.py:747
  93.9 2.7 %copy.5 = bf16[384,2048]{1,0:T(8,128)(2,1)} copy(bf16[384,2048]{1,0:T(8,128)(2,1)} %shard_map.37) | data formatting | bytes 3145728

commit v5 on v4

--- a/solution.py
+++ b/solution.py
@@ -281,7 +281,7 @@
     c_own.start()
 
     load.wait()
-    part = 16
+    part = 32
     kept = pl.ds(pl.multiple_of(x * own + c * TILE, TILE), TILE)
     passed = pl.ds(pl.multiple_of(x * own + (1 - c) * TILE, TILE), TILE)
 

time: 96.9 us -> 96.9 us (level)
  no operation moved by 1% of the time
where the time goes in v5:
time: 96.9 us; the launch traced here: 96.6 us
  Pallas kernels  93.9 us (97%)
  local copies, waits for them, and re-layouts  2.73 us (3%)
    pallas_call x1, Pallas kernels, whole(): pl.pallas_call(functools.partial(whole_kernel, (groups, owners, tokens_he...  93.9 us
    unnamed x1, local copies, waits for them, and re-layouts  2.73 us

profile of v5, /device:TPU:0, one launch (start us, length us, event | category | flops | bytes accessed | tf_op | source)
XLA Modules:
  0.0 96.6 jit_solution(13278179322703892776)
XLA Ops:
  0.0 93.9 %shard_map.37 = bf16[384,2048]{1,0:T(8,128)(2,1)} custom-call(bf16[128,4096]{1,0:T(8,128)(2,1)} %hidden_ref.1, f32[1,4096]{1,0:T(1,128)} %bitcast.1, bf16[128,6144]{1,0:T(8,128)(2,1)} %cotangent_ref.1), custom_call_target="tpu_custom_call" | custom-call | tf_op jit(solution)/shard_map/pallas_call | solution.py:747
  93.9 2.7 %copy.5 = bf16[384,2048]{1,0:T(8,128)(2,1)} copy(bf16[384,2048]{1,0:T(8,128)(2,1)} %shard_map.37) | data formatting | bytes 3145728
